TPU v7x, 128 devices: a whole 4x4x4 slice. The times are simulated.
128 devices in a mesh: dp: 16 (over y_lo, z, core), tensor: 8 (over x, y_hi).
Axes of the slice: x: 4, y: 4 (y_hi: 2, y_lo: 2; y = y_hi * 2 + y_lo), z: 4, core: 2. Of those that a mesh axis runs over, the one named last changes fastest.
Arguments:
- queries: bfloat16 [16384, 4096], P('dp')
- keys: bfloat16 [16384, 4096], P('dp')
- projection: bfloat16 [4096, 1024], P(None, 'tensor'), may hold values from -0.09375 to 0.09375
- positives: int32 [16, 1024], P('dp'), may hold values from 0 to 1023, each once within a row
Outputs:
- pair_loss: float32 [16384], P(('dp', 'tensor'))
- grad_queries: float32 [16384, 1024], P(('dp', 'tensor'))
- grad_keys: float32 [16384, 1024], P(('dp', 'tensor'))
Inputs may be any that keep to these rules, and one draw needn't show every extreme that they name: Each row of positives holds every number of 0 to 1023 once.
All inputs are finite; a program needn't handle non-finite values.
Results may differ from a plain program's by a relative error of at most 0.0069.
Values may be sent and summed in bfloat16 or wider, within the bound.
No kernel may reach another device: no remote copies, remote signals or barrier semaphores. Data moves between devices by JAX's collectives and lax.ppermute only.
A program may use at most 128 MiB of HBM per device.

v0:
```python
import jax
import jax.numpy as jnp
from jax import lax
from jax.sharding import PartitionSpec as P

SCALE = 100.0
EPSILON = 1e-06


def shifted(value, axis, steps):
    count = lax.axis_size(axis)
    pairs = [(source, (source + steps) % count) for source in range(count)]
    return lax.ppermute(value, axis, pairs)


def combined_all(part, axis, combine):
    gathered = jax.tree.map(lambda a: lax.all_gather(a, axis), part)

    def take(source):
        return jax.tree.map(lambda a: lax.dynamic_index_in_dim(a, source, 0, False), gathered)

    return lax.fori_loop(
        1, lax.axis_size(axis), lambda source, state: combine(state, take(source)), take(0)
    )


def normalize(embedding):
    entries = embedding.astype(jnp.float32)
    magnitude = jnp.sqrt(jnp.sum(entries * entries, axis=1, keepdims=True) + EPSILON)
    return (entries / magnitude, magnitude)


def unnormalize(grad_unit, unit_rows, magnitude):
    return (
        grad_unit - unit_rows * jnp.sum(unit_rows * grad_unit, axis=1, keepdims=True)
    ) / magnitude


def similarity(queries_unit, key_block):
    return SCALE * lax.dot_general(
        queries_unit, key_block, (((1,), (1,)), ((), ())), preferred_element_type=jnp.float32
    )


def cycle_keys(block, offset):
    return shifted(block, "dp", offset)


def cycle_grads(partial_value, offset):
    return shifted(partial_value, "dp", offset)


def advance(keys_now, direction):
    result = cycle_keys(keys_now, direction)
    return result


def absorb(running, queries_unit, key_block):
    row_max, row_sum = running
    scores = similarity(queries_unit, key_block)
    new_max = jnp.maximum(row_max, jnp.max(scores, axis=1))
    row_sum = row_sum * jnp.exp(row_max - new_max) + jnp.sum(
        jnp.exp(scores - new_max[:, None]), axis=1
    )
    return (new_max, row_sum)


def combine(earlier, latter):
    new_max = jnp.maximum(earlier[0], latter[0])
    row_sum = earlier[1] * jnp.exp(earlier[0] - new_max) + latter[1] * jnp.exp(latter[0] - new_max)
    return (new_max, row_sum, earlier[2] + latter[2])


def contributions(queries_unit, key_block, log_total, positive_mask):
    scores = similarity(queries_unit, key_block)
    weights = (jnp.exp(scores - log_total[:, None]) - positive_mask).astype(jnp.bfloat16)
    grad_q = SCALE * jnp.dot(weights, key_block, preferred_element_type=jnp.float32)
    grad_k = SCALE * lax.dot_general(
        weights, queries_unit, (((0,), (0,)), ((), ())), preferred_element_type=jnp.float32
    )
    return (grad_q, grad_k)


def body(queries, keys, projection, positives):
    query_count = queries.shape[0]
    group_count = lax.axis_size("tensor")
    cycle_count = lax.axis_size("dp")
    group_index = lax.axis_index("tensor")
    key_rows = query_count // group_count
    query_part = jnp.dot(queries, projection, preferred_element_type=jnp.float32).astype(
        jnp.bfloat16
    )
    key_part = jnp.dot(keys, projection, preferred_element_type=jnp.float32).astype(jnp.bfloat16)
    query_full, key_full = (
        lax.all_gather(query_part, "tensor", axis=1, tiled=True),
        lax.all_gather(key_part, "tensor", axis=1, tiled=True),
    )
    query_unit, query_mag = normalize(query_full)
    queries_unit = query_unit.astype(jnp.bfloat16)
    row_start = group_index * key_rows
    key_unit, key_mag = normalize(lax.dynamic_slice_in_dim(key_full, row_start, key_rows, 0))
    key_block = key_unit.astype(jnp.bfloat16)
    target = positives[0] - row_start
    positive_mask = (
        lax.broadcasted_iota(jnp.int32, (query_count, key_rows), 1) == target[:, None]
    ).astype(jnp.float32)
    own_scores = similarity(queries_unit, key_block)
    row_max = jnp.max(own_scores, axis=1)
    row_sum = jnp.sum(jnp.exp(own_scores - row_max[:, None]), axis=1)
    matched = jnp.sum(own_scores * positive_mask, axis=1)

    def step_ahead(keys_now):
        return advance(keys_now, 1)

    def sweep_one(turn_number, carried):
        forward_keys, running = carried
        forward_keys = step_ahead(forward_keys)
        return (forward_keys, absorb(running, queries_unit, forward_keys))

    forward_keys, running = lax.fori_loop(
        0, cycle_count - 1, sweep_one, (key_block, (row_max, row_sum))
    )
    row_max, row_sum, matched = combined_all((running[0], running[1], matched), "tensor", combine)
    log_total = row_max + jnp.log(row_sum)
    pair_loss = lax.dynamic_slice_in_dim(log_total - matched, row_start, key_rows, 0)
    grad_q, own_grad_k = contributions(queries_unit, key_block, log_total, positive_mask)

    def visit_one(turn_number, carried):
        forward_keys, forward_total, grad_sum = carried
        forward_keys = step_ahead(forward_keys)
        forward_total = cycle_grads(forward_total, 1)
        ahead_q, ahead_k = contributions(queries_unit, forward_keys, log_total, 0.0)
        return (forward_keys, forward_total + ahead_k, grad_sum + ahead_q)

    forward_keys, forward_total, grad_q = lax.fori_loop(
        0, cycle_count - 1, visit_one, (key_block, own_grad_k, grad_q)
    )
    grad_key_hat = cycle_grads(forward_total, 1)
    grad_rows = lax.psum_scatter(grad_q, "tensor", scatter_dimension=0, tiled=True)
    unit_rows = lax.dynamic_slice_in_dim(query_unit, row_start, key_rows, 0)
    magnitude_rows = lax.dynamic_slice_in_dim(query_mag, row_start, key_rows, 0)
    grad_queries = unnormalize(grad_rows, unit_rows, magnitude_rows)
    grad_keys = unnormalize(grad_key_hat, key_unit, key_mag)
    return (pair_loss, grad_queries, grad_keys)


def solution(mesh):
    in_specs = (P("dp", None), P("dp", None), P(None, "tensor"), P("dp", None))
    out_specs = (P(("dp", "tensor")), P(("dp", "tensor"), None), P(("dp", "tensor"), None))
    return jax.shard_map(body, mesh=mesh, in_specs=in_specs, out_specs=out_specs, check_vma=False)
```

profile of v0, /device:TPU:0, one launch (start us, length us, event | category | flops | bytes accessed | tf_op | source)
XLA Modules:
  0.0 744.4 jit_solution(18013519537378119752)
XLA Ops:
  21.4 53.0 %all-gather.8.cloned.1.call-done = bf16[1024,1024]{1,0:T(8,128)(2,1)} async-done(((bf16[1024,128]{1,0:T(8,128)(2,1)}), bf16[1024,1024]{1,0:T(8,128)(2,1)}) %all-gather.8.cloned.1.call-update) | async-done | bytes 2097168 | tf_op jit(solution)/shard_map/all_gather | solution.py:95
  76.4 56.4 %all-gather.6.cloned.1.call-done = bf16[1024,1024]{1,0:T(8,128)(2,1)} async-done(((bf16[1024,128]{1,0:T(8,128)(2,1)}), bf16[1024,1024]{1,0:T(8,128)(2,1)}) %all-gather.6.cloned.1.call-update) | async-done | bytes 2097168 | tf_op jit(solution)/shard_map/all_gather | solution.py:96
  144.5 147.2 %while.47 = (s32[]{:T(128)}, bf16[128,1024]{1,0:T(8,128)(2,1)}, f32[1024]{0:T(1024)S(1)}, f32[1024]{0:T(1024)S(1)}, bf16[1024,1024]{1,0:T(8,128)(2,1)S(1)}, /*index=5*/s32[]{:T(128)}) while((s32[]{:T(128)}, bf16[128,1024]{1,0:T(8,128)(2,1)}, f32[1024]{0:T(1024)S(1)}, f32[1024]{0:T(1024)S(1)}, bf16[1024,1024]{1,0:T(8,128)(2,1)S(1)}, ...), condition=%wide.region_7.8_spmd, body=%wide.region_4.7_spmd.sunk | while | flops 268961792 | bytes 5034093 | solution.py:120
  154.4 8.1 %collective-permute-done = bf16[128,1024]{1,0:T(8,128)(2,1)S(1)} collective-permute-done((bf16[128,1024]{1,0:T(8,128)(2,1)}, bf16[128,1024]{1,0:T(8,128)(2,1)S(1)}, u32[]{:S(2)}, u32[]{:S(2)}) %collective-permute-start) | collective-permute-done | bytes 262176 | tf_op jit(solution)/shard_map/while/body/eval_jaxpr/ppermute | solution.py:13
  164.2 8.1 %collective-permute-done = bf16[128,1024]{1,0:T(8,128)(2,1)S(1)} collective-permute-done((bf16[128,1024]{1,0:T(8,128)(2,1)}, bf16[128,1024]{1,0:T(8,128)(2,1)S(1)}, u32[]{:S(2)}, u32[]{:S(2)}) %collective-permute-start) | collective-permute-done | bytes 262176 | tf_op jit(solution)/shard_map/while/body/eval_jaxpr/ppermute | solution.py:13
  174.0 8.1 %collective-permute-done = bf16[128,1024]{1,0:T(8,128)(2,1)S(1)} collective-permute-done((bf16[128,1024]{1,0:T(8,128)(2,1)}, bf16[128,1024]{1,0:T(8,128)(2,1)S(1)}, u32[]{:S(2)}, u32[]{:S(2)}) %collective-permute-start) | collective-permute-done | bytes 262176 | tf_op jit(solution)/shard_map/while/body/eval_jaxpr/ppermute | solution.py:13
  183.8 8.1 %collective-permute-done = bf16[128,1024]{1,0:T(8,128)(2,1)S(1)} collective-permute-done((bf16[128,1024]{1,0:T(8,128)(2,1)}, bf16[128,1024]{1,0:T(8,128)(2,1)S(1)}, u32[]{:S(2)}, u32[]{:S(2)}) %collective-permute-start) | collective-permute-done | bytes 262176 | tf_op jit(solution)/shard_map/while/body/eval_jaxpr/ppermute | solution.py:13
  193.6 8.1 %collective-permute-done = bf16[128,1024]{1,0:T(8,128)(2,1)S(1)} collective-permute-done((bf16[128,1024]{1,0:T(8,128)(2,1)}, bf16[128,1024]{1,0:T(8,128)(2,1)S(1)}, u32[]{:S(2)}, u32[]{:S(2)}) %collective-permute-start) | collective-permute-done | bytes 262176 | tf_op jit(solution)/shard_map/while/body/eval_jaxpr/ppermute | solution.py:13
  203.4 8.1 %collective-permute-done = bf16[128,1024]{1,0:T(8,128)(2,1)S(1)} collective-permute-done((bf16[128,1024]{1,0:T(8,128)(2,1)}, bf16[128,1024]{1,0:T(8,128)(2,1)S(1)}, u32[]{:S(2)}, u32[]{:S(2)}) %collective-permute-start) | collective-permute-done | bytes 262176 | tf_op jit(solution)/shard_map/while/body/eval_jaxpr/ppermute | solution.py:13
  213.2 8.1 %collective-permute-done = bf16[128,1024]{1,0:T(8,128)(2,1)S(1)} collective-permute-done((bf16[128,1024]{1,0:T(8,128)(2,1)}, bf16[128,1024]{1,0:T(8,128)(2,1)S(1)}, u32[]{:S(2)}, u32[]{:S(2)}) %collective-permute-start) | collective-permute-done | bytes 262176 | tf_op jit(solution)/shard_map/while/body/eval_jaxpr/ppermute | solution.py:13
  223.0 8.1 %collective-permute-done = bf16[128,1024]{1,0:T(8,128)(2,1)S(1)} collective-permute-done((bf16[128,1024]{1,0:T(8,128)(2,1)}, bf16[128,1024]{1,0:T(8,128)(2,1)S(1)}, u32[]{:S(2)}, u32[]{:S(2)}) %collective-permute-start) | collective-permute-done | bytes 262176 | tf_op jit(solution)/shard_map/while/body/eval_jaxpr/ppermute | solution.py:13
  232.8 8.1 %collective-permute-done = bf16[128,1024]{1,0:T(8,128)(2,1)S(1)} collective-permute-done((bf16[128,1024]{1,0:T(8,128)(2,1)}, bf16[128,1024]{1,0:T(8,128)(2,1)S(1)}, u32[]{:S(2)}, u32[]{:S(2)}) %collective-permute-start) | collective-permute-done | bytes 262176 | tf_op jit(solution)/shard_map/while/body/eval_jaxpr/ppermute | solution.py:13
  242.6 8.1 %collective-permute-done = bf16[128,1024]{1,0:T(8,128)(2,1)S(1)} collective-permute-done((bf16[128,1024]{1,0:T(8,128)(2,1)}, bf16[128,1024]{1,0:T(8,128)(2,1)S(1)}, u32[]{:S(2)}, u32[]{:S(2)}) %collective-permute-start) | collective-permute-done | bytes 262176 | tf_op jit(solution)/shard_map/while/body/eval_jaxpr/ppermute | solution.py:13
  252.4 8.1 %collective-permute-done = bf16[128,1024]{1,0:T(8,128)(2,1)S(1)} collective-permute-done((bf16[128,1024]{1,0:T(8,128)(2,1)}, bf16[128,1024]{1,0:T(8,128)(2,1)S(1)}, u32[]{:S(2)}, u32[]{:S(2)}) %collective-permute-start) | collective-permute-done | bytes 262176 | tf_op jit(solution)/shard_map/while/body/eval_jaxpr/ppermute | solution.py:13
  262.2 8.1 %collective-permute-done = bf16[128,1024]{1,0:T(8,128)(2,1)S(1)} collective-permute-done((bf16[128,1024]{1,0:T(8,128)(2,1)}, bf16[128,1024]{1,0:T(8,128)(2,1)S(1)}, u32[]{:S(2)}, u32[]{:S(2)}) %collective-permute-start) | collective-permute-done | bytes 262176 | tf_op jit(solution)/shard_map/while/body/eval_jaxpr/ppermute | solution.py:13
  272.1 8.1 %collective-permute-done = bf16[128,1024]{1,0:T(8,128)(2,1)S(1)} collective-permute-done((bf16[128,1024]{1,0:T(8,128)(2,1)}, bf16[128,1024]{1,0:T(8,128)(2,1)S(1)}, u32[]{:S(2)}, u32[]{:S(2)}) %collective-permute-start) | collective-permute-done | bytes 262176 | tf_op jit(solution)/shard_map/while/body/eval_jaxpr/ppermute | solution.py:13
  281.9 8.2 %collective-permute-done = bf16[128,1024]{1,0:T(8,128)(2,1)S(1)} collective-permute-done((bf16[128,1024]{1,0:T(8,128)(2,1)}, bf16[128,1024]{1,0:T(8,128)(2,1)S(1)}, u32[]{:S(2)}, u32[]{:S(2)}) %collective-permute-start) | collective-permute-done | bytes 262176 | tf_op jit(solution)/shard_map/while/body/eval_jaxpr/ppermute | solution.py:13
  291.7 34.3 %all-gather = f32[8192]{0:T(1024)S(1)} all-gather(f32[1024]{0:T(1024)S(1)} %get-tuple-element.242), channel_id=2, replica_groups=mesh['dp'=16,'tensor'=8] {'tensor'}, dimensions={0}, use_global_device_ids=true | all-gather | bytes 36864 | tf_op jit(solution)/shard_map/all_gather | solution.py:17
  326.0 34.3 %all-gather.2 = f32[8192]{0:T(1024)S(1)} all-gather(f32[1024]{0:T(1024)S(1)} %get-tuple-element.249), channel_id=4, replica_groups=mesh['dp'=16,'tensor'=8] {'tensor'}, dimensions={0}, use_global_device_ids=true | all-gather | bytes 36864 | tf_op jit(solution)/shard_map/all_gather | solution.py:17
  360.3 34.3 %all-gather.1 = f32[8192]{0:T(1024)S(1)} all-gather(f32[1024]{0:T(1024)S(1)} %get-tuple-element.243), channel_id=3, replica_groups=mesh['dp'=16,'tensor'=8] {'tensor'}, dimensions={0}, use_global_device_ids=true | all-gather | bytes 36864 | tf_op jit(solution)/shard_map/all_gather | solution.py:17
  401.4 251.0 %while.49 = (s32[]{:T(128)}, bf16[128,1024]{1,0:T(8,128)(2,1)}, f32[128,1024]{1,0:T(8,128)}, f32[1024,1024]{1,0:T(8,128)}, bf16[1024,1024]{1,0:T(8,128)(2,1)S(1)}, /*index=5*/f32[1024]{0:T(1024)S(1)}, s32[]{:T(128)}) while((s32[]{:T(128)}, bf16[128,1024]{1,0:T(8,128)(2,1)}, f32[128,1024]{1,0:T(8,128)}, f32[1024,1024]{1,0:T(8,128)}, ...), condition=%wide.region_12.13_spmd, body=%wide.region_11.12_spmd.sunk | while | flops 808058880 | bytes 18616476 | solution.py:135
  401.4 8.1 %collective-permute-done.1 = bf16[128,1024]{1,0:T(8,128)(2,1)S(1)} collective-permute-done((bf16[128,1024]{1,0:T(8,128)(2,1)}, bf16[128,1024]{1,0:T(8,128)(2,1)S(1)}, u32[]{:S(2)}, u32[]{:S(2)}) %collective-permute-start.1) | collective-permute-done | bytes 262176 | tf_op jit(solution)/shard_map/while/body/eval_jaxpr/ppermute | solution.py:13
  418.1 8.1 %collective-permute-done.1 = bf16[128,1024]{1,0:T(8,128)(2,1)S(1)} collective-permute-done((bf16[128,1024]{1,0:T(8,128)(2,1)}, bf16[128,1024]{1,0:T(8,128)(2,1)S(1)}, u32[]{:S(2)}, u32[]{:S(2)}) %collective-permute-start.1) | collective-permute-done | bytes 262176 | tf_op jit(solution)/shard_map/while/body/eval_jaxpr/ppermute | solution.py:13
  451.6 8.1 %collective-permute-done.1 = bf16[128,1024]{1,0:T(8,128)(2,1)S(1)} collective-permute-done((bf16[128,1024]{1,0:T(8,128)(2,1)}, bf16[128,1024]{1,0:T(8,128)(2,1)S(1)}, u32[]{:S(2)}, u32[]{:S(2)}) %collective-permute-start.1) | collective-permute-done | bytes 262176 | tf_op jit(solution)/shard_map/while/body/eval_jaxpr/ppermute | solution.py:13
  535.2 8.1 %collective-permute-done.1 = bf16[128,1024]{1,0:T(8,128)(2,1)S(1)} collective-permute-done((bf16[128,1024]{1,0:T(8,128)(2,1)}, bf16[128,1024]{1,0:T(8,128)(2,1)S(1)}, u32[]{:S(2)}, u32[]{:S(2)}) %collective-permute-start.1) | collective-permute-done | bytes 262176 | tf_op jit(solution)/shard_map/while/body/eval_jaxpr/ppermute | solution.py:13
  552.0 8.1 %collective-permute-done.1 = bf16[128,1024]{1,0:T(8,128)(2,1)S(1)} collective-permute-done((bf16[128,1024]{1,0:T(8,128)(2,1)}, bf16[128,1024]{1,0:T(8,128)(2,1)S(1)}, u32[]{:S(2)}, u32[]{:S(2)}) %collective-permute-start.1) | collective-permute-done | bytes 262176 | tf_op jit(solution)/shard_map/while/body/eval_jaxpr/ppermute | solution.py:13
  568.7 8.1 %collective-permute-done.1 = bf16[128,1024]{1,0:T(8,128)(2,1)S(1)} collective-permute-done((bf16[128,1024]{1,0:T(8,128)(2,1)}, bf16[128,1024]{1,0:T(8,128)(2,1)S(1)}, u32[]{:S(2)}, u32[]{:S(2)}) %collective-permute-start.1) | collective-permute-done | bytes 262176 | tf_op jit(solution)/shard_map/while/body/eval_jaxpr/ppermute | solution.py:13
  585.4 8.1 %collective-permute-done.1 = bf16[128,1024]{1,0:T(8,128)(2,1)S(1)} collective-permute-done((bf16[128,1024]{1,0:T(8,128)(2,1)}, bf16[128,1024]{1,0:T(8,128)(2,1)S(1)}, u32[]{:S(2)}, u32[]{:S(2)}) %collective-permute-start.1) | collective-permute-done | bytes 262176 | tf_op jit(solution)/shard_map/while/body/eval_jaxpr/ppermute | solution.py:13
  602.2 8.1 %collective-permute-done.1 = bf16[128,1024]{1,0:T(8,128)(2,1)S(1)} collective-permute-done((bf16[128,1024]{1,0:T(8,128)(2,1)}, bf16[128,1024]{1,0:T(8,128)(2,1)S(1)}, u32[]{:S(2)}, u32[]{:S(2)}) %collective-permute-start.1) | collective-permute-done | bytes 262176 | tf_op jit(solution)/shard_map/while/body/eval_jaxpr/ppermute | solution.py:13
  618.9 8.1 %collective-permute-done.1 = bf16[128,1024]{1,0:T(8,128)(2,1)S(1)} collective-permute-done((bf16[128,1024]{1,0:T(8,128)(2,1)}, bf16[128,1024]{1,0:T(8,128)(2,1)S(1)}, u32[]{:S(2)}, u32[]{:S(2)}) %collective-permute-start.1) | collective-permute-done | bytes 262176 | tf_op jit(solution)/shard_map/while/body/eval_jaxpr/ppermute | solution.py:13
  654.1 13.7 %collective-permute-done.3 = f32[128,1024]{1,0:T(8,128)S(1)} collective-permute-done((f32[128,1024]{1,0:T(8,128)S(1)}, f32[128,1024]{1,0:T(8,128)S(1)}, u32[]{:S(2)}, u32[]{:S(2)}) %collective-permute-start.3) | collective-permute-done | bytes 524320 | tf_op jit(solution)/shard_map/ppermute | solution.py:13
  670.9 63.6 %reduce-scatter.2.cloned.1.call-done = f32[128,1024]{1,0:T(8,128)} async-done(((f32[1024,1024]{1,0:T(8,128)}), f32[128,1024]{1,0:T(8,128)}) %reduce-scatter.2.cloned.1.call-update) | async-done | bytes 524304 | tf_op jit(solution)/shard_map/reduce_scatter | solution.py:139
  (288 shorter events, 254.1 us)
Async XLA Ops:
  7.2 67.2 %all-gather.8.cloned.1.call-start = ((), (), s32[]{:S(2)}) async-start(), calls=%async_computation.2 | async-start | bytes 2359296 | tf_op jit(solution)/shard_map/all_gather | solution.py:95
  14.8 118.0 %all-gather.6.cloned.1.call-start = ((), (), s32[]{:S(2)}) async-start(), calls=%async_computation.1 | async-start | bytes 2359296 | tf_op jit(solution)/shard_map/all_gather | solution.py:96
  21.3 713.1 %reduce-scatter.2.cloned.1.call-start = ((), (), s32[]{:S(2)}) async-start(), calls=%async_computation.3 | async-start | bytes 4718592 | tf_op jit(solution)/shard_map/reduce_scatter | solution.py:139
  144.5 8.2 %collective-permute-start = (bf16[128,1024]{1,0:T(8,128)(2,1)}, bf16[128,1024]{1,0:T(8,128)(2,1)S(1)}, u32[]{:S(2)}, u32[]{:S(2)}) collective-permute-start(bf16[128,1024]{1,0:T(8,128)(2,1)} %get-tuple-element.429), channel_id=1, source_target_pairs={{0,8},{8,16},{16,24},{24,32},{32,40},{40,48},{48,56},{56,64},{64,7... | collective-permute-start | bytes 786440 | tf_op jit(solution)/shard_map/while/body/eval_jaxpr/ppermute | solution.py:13
  164.2 8.1 %collective-permute-start = (bf16[128,1024]{1,0:T(8,128)(2,1)}, bf16[128,1024]{1,0:T(8,128)(2,1)S(1)}, u32[]{:S(2)}, u32[]{:S(2)}) collective-permute-start(bf16[128,1024]{1,0:T(8,128)(2,1)} %get-tuple-element.429), channel_id=1, source_target_pairs={{0,8},{8,16},{16,24},{24,32},{32,40},{40,48},{48,56},{56,64},{64,7... | collective-permute-start | bytes 786440 | tf_op jit(solution)/shard_map/while/body/eval_jaxpr/ppermute | solution.py:13
  193.6 8.1 %collective-permute-start = (bf16[128,1024]{1,0:T(8,128)(2,1)}, bf16[128,1024]{1,0:T(8,128)(2,1)S(1)}, u32[]{:S(2)}, u32[]{:S(2)}) collective-permute-start(bf16[128,1024]{1,0:T(8,128)(2,1)} %get-tuple-element.429), channel_id=1, source_target_pairs={{0,8},{8,16},{16,24},{24,32},{32,40},{40,48},{48,56},{56,64},{64,7... | collective-permute-start | bytes 786440 | tf_op jit(solution)/shard_map/while/body/eval_jaxpr/ppermute | solution.py:13
  203.4 8.1 %collective-permute-start = (bf16[128,1024]{1,0:T(8,128)(2,1)}, bf16[128,1024]{1,0:T(8,128)(2,1)S(1)}, u32[]{:S(2)}, u32[]{:S(2)}) collective-permute-start(bf16[128,1024]{1,0:T(8,128)(2,1)} %get-tuple-element.429), channel_id=1, source_target_pairs={{0,8},{8,16},{16,24},{24,32},{32,40},{40,48},{48,56},{56,64},{64,7... | collective-permute-start | bytes 786440 | tf_op jit(solution)/shard_map/while/body/eval_jaxpr/ppermute | solution.py:13
  232.8 8.1 %collective-permute-start = (bf16[128,1024]{1,0:T(8,128)(2,1)}, bf16[128,1024]{1,0:T(8,128)(2,1)S(1)}, u32[]{:S(2)}, u32[]{:S(2)}) collective-permute-start(bf16[128,1024]{1,0:T(8,128)(2,1)} %get-tuple-element.429), channel_id=1, source_target_pairs={{0,8},{8,16},{16,24},{24,32},{32,40},{40,48},{48,56},{56,64},{64,7... | collective-permute-start | bytes 786440 | tf_op jit(solution)/shard_map/while/body/eval_jaxpr/ppermute | solution.py:13
  242.6 8.1 %collective-permute-start = (bf16[128,1024]{1,0:T(8,128)(2,1)}, bf16[128,1024]{1,0:T(8,128)(2,1)S(1)}, u32[]{:S(2)}, u32[]{:S(2)}) collective-permute-start(bf16[128,1024]{1,0:T(8,128)(2,1)} %get-tuple-element.429), channel_id=1, source_target_pairs={{0,8},{8,16},{16,24},{24,32},{32,40},{40,48},{48,56},{56,64},{64,7... | collective-permute-start | bytes 786440 | tf_op jit(solution)/shard_map/while/body/eval_jaxpr/ppermute | solution.py:13
  272.1 8.1 %collective-permute-start = (bf16[128,1024]{1,0:T(8,128)(2,1)}, bf16[128,1024]{1,0:T(8,128)(2,1)S(1)}, u32[]{:S(2)}, u32[]{:S(2)}) collective-permute-start(bf16[128,1024]{1,0:T(8,128)(2,1)} %get-tuple-element.429), channel_id=1, source_target_pairs={{0,8},{8,16},{16,24},{24,32},{32,40},{40,48},{48,56},{56,64},{64,7... | collective-permute-start | bytes 786440 | tf_op jit(solution)/shard_map/while/body/eval_jaxpr/ppermute | solution.py:13
  281.9 8.2 %collective-permute-start = (bf16[128,1024]{1,0:T(8,128)(2,1)}, bf16[128,1024]{1,0:T(8,128)(2,1)S(1)}, u32[]{:S(2)}, u32[]{:S(2)}) collective-permute-start(bf16[128,1024]{1,0:T(8,128)(2,1)} %get-tuple-element.429), channel_id=1, source_target_pairs={{0,8},{8,16},{16,24},{24,32},{32,40},{40,48},{48,56},{56,64},{64,7... | collective-permute-start | bytes 786440 | tf_op jit(solution)/shard_map/while/body/eval_jaxpr/ppermute | solution.py:13
  401.4 14.4 %collective-permute-start.2 = (f32[128,1024]{1,0:T(8,128)}, f32[128,1024]{1,0:T(8,128)}, u32[]{:S(2)}, u32[]{:S(2)}) collective-permute-start(f32[128,1024]{1,0:T(8,128)} %get-tuple-element.479), channel_id=1, source_target_pairs={{0,8},{8,16},{16,24},{24,32},{32,40},{40,48},{48,56},{56,64},{64,7... | collective-permute-start | bytes 1572872 | tf_op jit(solution)/shard_map/while/body/eval_jaxpr/ppermute | solution.py:13
  418.1 8.1 %collective-permute-start.1 = (bf16[128,1024]{1,0:T(8,128)(2,1)}, bf16[128,1024]{1,0:T(8,128)(2,1)S(1)}, u32[]{:S(2)}, u32[]{:S(2)}) collective-permute-start(bf16[128,1024]{1,0:T(8,128)(2,1)} %get-tuple-element.478), channel_id=1, source_target_pairs={{0,8},{8,16},{16,24},{24,32},{32,40},{40,48},{48,56},{56,64},{64,7... | collective-permute-start | bytes 786440 | tf_op jit(solution)/shard_map/while/body/eval_jaxpr/ppermute | solution.py:13
  418.1 14.4 %collective-permute-start.2 = (f32[128,1024]{1,0:T(8,128)}, f32[128,1024]{1,0:T(8,128)}, u32[]{:S(2)}, u32[]{:S(2)}) collective-permute-start(f32[128,1024]{1,0:T(8,128)} %get-tuple-element.479), channel_id=1, source_target_pairs={{0,8},{8,16},{16,24},{24,32},{32,40},{40,48},{48,56},{56,64},{64,7... | collective-permute-start | bytes 1572872 | tf_op jit(solution)/shard_map/while/body/eval_jaxpr/ppermute | solution.py:13
  434.8 14.4 %collective-permute-start.2 = (f32[128,1024]{1,0:T(8,128)}, f32[128,1024]{1,0:T(8,128)}, u32[]{:S(2)}, u32[]{:S(2)}) collective-permute-start(f32[128,1024]{1,0:T(8,128)} %get-tuple-element.479), channel_id=1, source_target_pairs={{0,8},{8,16},{16,24},{24,32},{32,40},{40,48},{48,56},{56,64},{64,7... | collective-permute-start | bytes 1572872 | tf_op jit(solution)/shard_map/while/body/eval_jaxpr/ppermute | solution.py:13
  451.6 14.4 %collective-permute-start.2 = (f32[128,1024]{1,0:T(8,128)}, f32[128,1024]{1,0:T(8,128)}, u32[]{:S(2)}, u32[]{:S(2)}) collective-permute-start(f32[128,1024]{1,0:T(8,128)} %get-tuple-element.479), channel_id=1, source_target_pairs={{0,8},{8,16},{16,24},{24,32},{32,40},{40,48},{48,56},{56,64},{64,7... | collective-permute-start | bytes 1572872 | tf_op jit(solution)/shard_map/while/body/eval_jaxpr/ppermute | solution.py:13
  468.3 14.4 %collective-permute-start.2 = (f32[128,1024]{1,0:T(8,128)}, f32[128,1024]{1,0:T(8,128)}, u32[]{:S(2)}, u32[]{:S(2)}) collective-permute-start(f32[128,1024]{1,0:T(8,128)} %get-tuple-element.479), channel_id=1, source_target_pairs={{0,8},{8,16},{16,24},{24,32},{32,40},{40,48},{48,56},{56,64},{64,7... | collective-permute-start | bytes 1572872 | tf_op jit(solution)/shard_map/while/body/eval_jaxpr/ppermute | solution.py:13
  485.0 14.4 %collective-permute-start.2 = (f32[128,1024]{1,0:T(8,128)}, f32[128,1024]{1,0:T(8,128)}, u32[]{:S(2)}, u32[]{:S(2)}) collective-permute-start(f32[128,1024]{1,0:T(8,128)} %get-tuple-element.479), channel_id=1, source_target_pairs={{0,8},{8,16},{16,24},{24,32},{32,40},{40,48},{48,56},{56,64},{64,7... | collective-permute-start | bytes 1572872 | tf_op jit(solution)/shard_map/while/body/eval_jaxpr/ppermute | solution.py:13
  501.8 14.4 %collective-permute-start.2 = (f32[128,1024]{1,0:T(8,128)}, f32[128,1024]{1,0:T(8,128)}, u32[]{:S(2)}, u32[]{:S(2)}) collective-permute-start(f32[128,1024]{1,0:T(8,128)} %get-tuple-element.479), channel_id=1, source_target_pairs={{0,8},{8,16},{16,24},{24,32},{32,40},{40,48},{48,56},{56,64},{64,7... | collective-permute-start | bytes 1572872 | tf_op jit(solution)/shard_map/while/body/eval_jaxpr/ppermute | solution.py:13
  518.5 14.4 %collective-permute-start.2 = (f32[128,1024]{1,0:T(8,128)}, f32[128,1024]{1,0:T(8,128)}, u32[]{:S(2)}, u32[]{:S(2)}) collective-permute-start(f32[128,1024]{1,0:T(8,128)} %get-tuple-element.479), channel_id=1, source_target_pairs={{0,8},{8,16},{16,24},{24,32},{32,40},{40,48},{48,56},{56,64},{64,7... | collective-permute-start | bytes 1572872 | tf_op jit(solution)/shard_map/while/body/eval_jaxpr/ppermute | solution.py:13
  535.2 8.1 %collective-permute-start.1 = (bf16[128,1024]{1,0:T(8,128)(2,1)}, bf16[128,1024]{1,0:T(8,128)(2,1)S(1)}, u32[]{:S(2)}, u32[]{:S(2)}) collective-permute-start(bf16[128,1024]{1,0:T(8,128)(2,1)} %get-tuple-element.478), channel_id=1, source_target_pairs={{0,8},{8,16},{16,24},{24,32},{32,40},{40,48},{48,56},{56,64},{64,7... | collective-permute-start | bytes 786440 | tf_op jit(solution)/shard_map/while/body/eval_jaxpr/ppermute | solution.py:13
  535.2 14.4 %collective-permute-start.2 = (f32[128,1024]{1,0:T(8,128)}, f32[128,1024]{1,0:T(8,128)}, u32[]{:S(2)}, u32[]{:S(2)}) collective-permute-start(f32[128,1024]{1,0:T(8,128)} %get-tuple-element.479), channel_id=1, source_target_pairs={{0,8},{8,16},{16,24},{24,32},{32,40},{40,48},{48,56},{56,64},{64,7... | collective-permute-start | bytes 1572872 | tf_op jit(solution)/shard_map/while/body/eval_jaxpr/ppermute | solution.py:13
  552.0 8.1 %collective-permute-start.1 = (bf16[128,1024]{1,0:T(8,128)(2,1)}, bf16[128,1024]{1,0:T(8,128)(2,1)S(1)}, u32[]{:S(2)}, u32[]{:S(2)}) collective-permute-start(bf16[128,1024]{1,0:T(8,128)(2,1)} %get-tuple-element.478), channel_id=1, source_target_pairs={{0,8},{8,16},{16,24},{24,32},{32,40},{40,48},{48,56},{56,64},{64,7... | collective-permute-start | bytes 786440 | tf_op jit(solution)/shard_map/while/body/eval_jaxpr/ppermute | solution.py:13
  552.0 14.4 %collective-permute-start.2 = (f32[128,1024]{1,0:T(8,128)}, f32[128,1024]{1,0:T(8,128)}, u32[]{:S(2)}, u32[]{:S(2)}) collective-permute-start(f32[128,1024]{1,0:T(8,128)} %get-tuple-element.479), channel_id=1, source_target_pairs={{0,8},{8,16},{16,24},{24,32},{32,40},{40,48},{48,56},{56,64},{64,7... | collective-permute-start | bytes 1572872 | tf_op jit(solution)/shard_map/while/body/eval_jaxpr/ppermute | solution.py:13
  568.7 8.1 %collective-permute-start.1 = (bf16[128,1024]{1,0:T(8,128)(2,1)}, bf16[128,1024]{1,0:T(8,128)(2,1)S(1)}, u32[]{:S(2)}, u32[]{:S(2)}) collective-permute-start(bf16[128,1024]{1,0:T(8,128)(2,1)} %get-tuple-element.478), channel_id=1, source_target_pairs={{0,8},{8,16},{16,24},{24,32},{32,40},{40,48},{48,56},{56,64},{64,7... | collective-permute-start | bytes 786440 | tf_op jit(solution)/shard_map/while/body/eval_jaxpr/ppermute | solution.py:13
  568.7 14.4 %collective-permute-start.2 = (f32[128,1024]{1,0:T(8,128)}, f32[128,1024]{1,0:T(8,128)}, u32[]{:S(2)}, u32[]{:S(2)}) collective-permute-start(f32[128,1024]{1,0:T(8,128)} %get-tuple-element.479), channel_id=1, source_target_pairs={{0,8},{8,16},{16,24},{24,32},{32,40},{40,48},{48,56},{56,64},{64,7... | collective-permute-start | bytes 1572872 | tf_op jit(solution)/shard_map/while/body/eval_jaxpr/ppermute | solution.py:13
  585.4 8.1 %collective-permute-start.1 = (bf16[128,1024]{1,0:T(8,128)(2,1)}, bf16[128,1024]{1,0:T(8,128)(2,1)S(1)}, u32[]{:S(2)}, u32[]{:S(2)}) collective-permute-start(bf16[128,1024]{1,0:T(8,128)(2,1)} %get-tuple-element.478), channel_id=1, source_target_pairs={{0,8},{8,16},{16,24},{24,32},{32,40},{40,48},{48,56},{56,64},{64,7... | collective-permute-start | bytes 786440 | tf_op jit(solution)/shard_map/while/body/eval_jaxpr/ppermute | solution.py:13
  585.4 14.4 %collective-permute-start.2 = (f32[128,1024]{1,0:T(8,128)}, f32[128,1024]{1,0:T(8,128)}, u32[]{:S(2)}, u32[]{:S(2)}) collective-permute-start(f32[128,1024]{1,0:T(8,128)} %get-tuple-element.479), channel_id=1, source_target_pairs={{0,8},{8,16},{16,24},{24,32},{32,40},{40,48},{48,56},{56,64},{64,7... | collective-permute-start | bytes 1572872 | tf_op jit(solution)/shard_map/while/body/eval_jaxpr/ppermute | solution.py:13
  602.2 14.4 %collective-permute-start.2 = (f32[128,1024]{1,0:T(8,128)}, f32[128,1024]{1,0:T(8,128)}, u32[]{:S(2)}, u32[]{:S(2)}) collective-permute-start(f32[128,1024]{1,0:T(8,128)} %get-tuple-element.479), channel_id=1, source_target_pairs={{0,8},{8,16},{16,24},{24,32},{32,40},{40,48},{48,56},{56,64},{64,7... | collective-permute-start | bytes 1572872 | tf_op jit(solution)/shard_map/while/body/eval_jaxpr/ppermute | solution.py:13
  618.9 14.4 %collective-permute-start.2 = (f32[128,1024]{1,0:T(8,128)}, f32[128,1024]{1,0:T(8,128)}, u32[]{:S(2)}, u32[]{:S(2)}) collective-permute-start(f32[128,1024]{1,0:T(8,128)} %get-tuple-element.479), channel_id=1, source_target_pairs={{0,8},{8,16},{16,24},{24,32},{32,40},{40,48},{48,56},{56,64},{64,7... | collective-permute-start | bytes 1572872 | tf_op jit(solution)/shard_map/while/body/eval_jaxpr/ppermute | solution.py:13
  635.6 14.4 %collective-permute-start.2 = (f32[128,1024]{1,0:T(8,128)}, f32[128,1024]{1,0:T(8,128)}, u32[]{:S(2)}, u32[]{:S(2)}) collective-permute-start(f32[128,1024]{1,0:T(8,128)} %get-tuple-element.479), channel_id=1, source_target_pairs={{0,8},{8,16},{16,24},{24,32},{32,40},{40,48},{48,56},{56,64},{64,7... | collective-permute-start | bytes 1572872 | tf_op jit(solution)/shard_map/while/body/eval_jaxpr/ppermute | solution.py:13
  653.4 14.4 %collective-permute-start.3 = (f32[128,1024]{1,0:T(8,128)S(1)}, f32[128,1024]{1,0:T(8,128)S(1)}, u32[]{:S(2)}, u32[]{:S(2)}) collective-permute-start(f32[128,1024]{1,0:T(8,128)S(1)} %copy-done.2), channel_id=1, source_target_pairs={{0,8},{8,16},{16,24},{24,32},{32,40},{40,48},{48,56},{56,64},{64,7... | collective-permute-start | bytes 1572872 | tf_op jit(solution)/shard_map/ppermute | solution.py:13
  (21 other events, 147.6 us)
Sparse Core Ops, SparseCore 0:
  15.0 59.3 all-gather.7
  77.1 55.6 all-gather.5
  652.5 81.8 reduce-scatter.1
where the time goes:
time: 746 us; the launch traced here: 744 us
  waiting for transfers between devices  430 us (58%)
  matrix products  152 us (20%)
  blocking collectives  103 us (14%)
  local copies, waits for them, and re-layouts  26.9 us (4%)
  other arithmetic  17.8 us (2%)
  between operations  13.8 us (2%)
    ppermute x46, waiting for transfers between devices, shifted(): return lax.ppermute(value, axis, pairs)  257 us
    all_gather x3, blocking collectives, combined_all(): gathered = jax.tree.map(lambda a: lax.all_gather(a, axis), part)  103 us
    dot_general x16, matrix products, contributions(): jnp.dot(weights, key_block, preferred_element_type=jnp.float32)  76.7 us
    reduce_scatter x1, waiting for transfers between devices, body(): lax.psum_scatter(grad_q, 'tensor', scatter_dimension=0, tiled=True)  63.6 us
    all_gather x1, waiting for transfers between devices, body(): lax.all_gather(key_part, 'tensor', axis=1, tiled=True)  56.4 us
    all_gather x1, waiting for transfers between devices, body(): lax.all_gather(query_part, 'tensor', axis=1, tiled=True)  53 us
    dot_general x16, matrix products, contributions(): lax.dot_general(weights, queries_unit, (((0,), (0,)), ((), ())), preferre...  37 us
    dot_general x31, matrix products, similarity(): lax.dot_general(queries_unit, key_block, (((1,), (1,)), ((), ())), prefer...  25.1 us
  transfers between devices with their start and end apart: 49, of which 34 were waited for; matrix products, arithmetic and copies ran while one was open for 14% of the time, Pallas kernels for 0%

commit v1 on v0

v1 whole, which is shorter than its diff:
```python
import jax
import jax.numpy as jnp
from jax import lax
from jax.sharding import PartitionSpec as P

SCALE = 100.0
EPSILON = 1e-06


def normalize(embedding):
    entries = embedding.astype(jnp.float32)
    magnitude = jnp.sqrt(jnp.sum(entries * entries, axis=1, keepdims=True) + EPSILON)
    return (entries / magnitude, magnitude)


def unnormalize(grad_unit, unit_rows, magnitude):
    return (
        grad_unit - unit_rows * jnp.sum(unit_rows * grad_unit, axis=1, keepdims=True)
    ) / magnitude


def body(queries, keys, projection, positives):
    rows = queries.shape[0]
    group_count = lax.axis_size("tensor")
    group_index = lax.axis_index("tensor")
    block_index = lax.axis_index("dp")
    slice_rows = rows // group_count
    row_start = group_index * slice_rows

    query_part = jnp.dot(queries, projection, preferred_element_type=jnp.float32).astype(jnp.bfloat16)
    key_part = jnp.dot(keys, projection, preferred_element_type=jnp.float32).astype(jnp.bfloat16)
    query_full = lax.all_gather(query_part, "tensor", axis=1, tiled=True)
    key_rows = lax.all_to_all(key_part, "tensor", 0, 1, tiled=True)

    query_unit, query_mag = normalize(query_full)
    queries_hat = query_unit.astype(jnp.bfloat16)
    key_unit, key_mag = normalize(key_rows)
    key_hat = key_unit.astype(jnp.bfloat16)
    keys_all = lax.all_gather(key_hat, "dp", axis=0, tiled=True)

    scores = SCALE * lax.dot_general(
        queries_hat, keys_all, (((1,), (1,)), ((), ())), preferred_element_type=jnp.float32
    )
    local_pos = positives[0] - row_start
    column = block_index * slice_rows + local_pos
    valid = (local_pos >= 0) & (local_pos < slice_rows)
    column = jnp.where(valid, column, -1)
    positive_mask = (
        lax.broadcasted_iota(jnp.int32, scores.shape, 1) == column[:, None]
    ).astype(jnp.float32)
    row_max = jnp.max(scores, axis=1)
    row_sum = jnp.sum(jnp.exp(scores - row_max[:, None]), axis=1)
    matched = jnp.sum(scores * positive_mask, axis=1)

    stats = lax.all_gather(jnp.stack([row_max, row_sum, matched]), "tensor", axis=0)
    all_max = jnp.max(stats[:, 0], axis=0)
    total = jnp.sum(stats[:, 1] * jnp.exp(stats[:, 0] - all_max[None, :]), axis=0)
    matched = jnp.sum(stats[:, 2], axis=0)
    log_total = all_max + jnp.log(total)
    pair_loss = lax.dynamic_slice_in_dim(log_total - matched, row_start, slice_rows, 0)

    weights = (jnp.exp(scores - log_total[:, None]) - positive_mask).astype(jnp.bfloat16)
    grad_k = SCALE * lax.dot_general(
        weights, queries_hat, (((0,), (0,)), ((), ())), preferred_element_type=jnp.float32
    )
    grad_key_hat = lax.psum_scatter(grad_k, "dp", scatter_dimension=0, tiled=True)
    grad_q = SCALE * jnp.dot(weights, keys_all, preferred_element_type=jnp.float32)
    grad_rows = lax.psum_scatter(grad_q, "tensor", scatter_dimension=0, tiled=True)

    unit_rows = lax.dynamic_slice_in_dim(query_unit, row_start, slice_rows, 0)
    magnitude_rows = lax.dynamic_slice_in_dim(query_mag, row_start, slice_rows, 0)
    grad_queries = unnormalize(grad_rows, unit_rows, magnitude_rows)
    grad_keys = unnormalize(grad_key_hat, key_unit, key_mag)
    return (pair_loss, grad_queries, grad_keys)


def solution(mesh):
    in_specs = (P("dp", None), P("dp", None), P(None, "tensor"), P("dp", None))
    out_specs = (P(("dp", "tensor")), P(("dp", "tensor"), None), P(("dp", "tensor"), None))
    return jax.shard_map(body, mesh=mesh, in_specs=in_specs, out_specs=out_specs, check_vma=False)
```

time: 746 us -> 339 us (0.45)
  waiting for transfers between devices: 430 us -> 216 us
  matrix products: 152 us -> 39.1 us
  blocking collectives: 103 us -> 51 us
  local copies, waits for them, and re-layouts: 26.9 us -> 1.85 us
    ppermute x46 -> x0, waiting for transfers between devices: 257 us -> none  [shifted(): return lax.ppermute(value, axis, pairs)]
    dot_general x63 -> x3, matrix products: 139 us -> 26.9 us  [the longest x1 12.6 us: body(): lax.dot_general(weights, queries_hat, (((0,), (0,)), ((), ())), preferred...]
    reduce_scatter x0 -> x1, waiting for transfers between devices: none -> 72.8 us  [body(): lax.psum_scatter(grad_k, 'dp', scatter_dimension=0, tiled=True)]
    all_gather x3 -> x1, blocking collectives: 103 us -> 34.3 us  [body(): lax.all_gather(jnp.stack([row_max, row_sum, matched]), 'tensor', axis=0)]
    all_gather x2, waiting for transfers between devices: 109 us -> 74.1 us  [the longest x1 37.7 us: body(): query_full = lax.all_gather(query_part, 'tensor', axis=1, tiled=True)]
    while x45 -> x0, local copies, waits for them, and re-layouts: 21.3 us -> none
    all_to_all x0 -> x1, blocking collectives: none -> 16.7 us  [body(): key_rows = lax.all_to_all(key_part, 'tensor', 0, 1, tiled=True)]
  transfers between devices with their start and end apart: 49 -> 4, of which waited for: 34 -> 4; matrix products, arithmetic and copies ran while one was open for 14% -> 8% of each run, Pallas kernels for 0% -> 0%
where the time goes in v1:
time: 339 us
  waiting for transfers between devices  216 us (64%)
  blocking collectives  51 us (15%)
  matrix products  39.1 us (12%)
  other arithmetic  16.8 us (5%)
  between operations  13.9 us (4%)
    reduce_scatter x1, waiting for transfers between devices, body(): lax.psum_scatter(grad_k, 'dp', scatter_dimension=0, tiled=True)  72.8 us
    reduce_scatter x1, waiting for transfers between devices, body(): lax.psum_scatter(grad_q, 'tensor', scatter_dimension=0, tiled=True)  68.8 us
    all_gather x1, waiting for transfers between devices, body(): query_full = lax.all_gather(query_part, 'tensor', axis=1, tiled=True)  37.7 us
    all_gather x1, waiting for transfers between devices, body(): keys_all = lax.all_gather(key_hat, 'dp', axis=0, tiled=True)  36.4 us
    all_gather x1, blocking collectives, body(): lax.all_gather(jnp.stack([row_max, row_sum, matched]), 'tensor', axis=0)  34.3 us
    all_to_all x1, blocking collectives, body(): key_rows = lax.all_to_all(key_part, 'tensor', 0, 1, tiled=True)  16.7 us
    dot_general x1, matrix products, body(): lax.dot_general(weights, queries_hat, (((0,), (0,)), ((), ())), preferred...  12.6 us
    dot_general x1, matrix products, body(): lax.dot_general(queries_hat, keys_all, (((1,), (1,)), ((), ())), preferre...  7.22 us
  transfers between devices with their start and end apart: 4, of which 4 were waited for; matrix products, arithmetic and copies ran while one was open for 8% of the time, Pallas kernels for 0%

profile of v1, /device:TPU:0, one launch (start us, length us, event | category | flops | bytes accessed | tf_op | source)
XLA Modules:
  0.0 338.7 jit_solution(4571559444627770995)
XLA Ops:
  7.2 0.0 all-gather.5.cloned.1.call-start
  7.2 1.2 copy-done
  8.4 6.4 %convolution_convert_fusion.1 = bf16[1024,128]{1,0:T(8,128)(2,1)} fusion(bf16[1024,4096]{1,0:T(8,128)(2,1)} %param.4, bf16[4096,128]{1,0:T(8,128)(2,1)S(1)} %copy-done), kind=kOutput, calls=%fused_computation.11 | convolution fusion | flops 1073872896 | bytes 9699328 | tf_op jit(solution)/shard_map/dot_general | solution.py:30
  14.8 0.0 all-gather.5.cloned.1.call-update
  14.8 0.0 all-gather.7.cloned.1.call-start
  14.9 5.7 %convolution_convert_fusion = bf16[1024,128]{1,0:T(8,128)(2,1)S(1)} fusion(bf16[1024,4096]{1,0:T(8,128)(2,1)} %param.5, bf16[4096,128]{1,0:T(8,128)(2,1)S(1)} %copy-done), kind=kOutput, calls=%fused_computation.10 | convolution fusion | flops 1073872896 | bytes 9699328 | tf_op jit(solution)/shard_map/dot_general | solution.py:31
  20.6 16.7 %all_to_all.13 = bf16[8,128,128]{2,1,0:T(8,128)(2,1)S(1)} all-to-all(bf16[8,128,128]{2,1,0:T(8,128)(2,1)S(1)} %bitcast.39), channel_id=1, replica_groups=mesh['dp'=16,'tensor'=8] {'tensor'}, dimensions={0} | all-to-all | bytes 524288 | tf_op jit(solution)/shard_map/all_to_all | solution.py:33
  37.3 0.1 fusion.4
  37.4 0.8 fusion.9
  38.2 0.0 all-gather.7.cloned.1.call-update
  38.3 0.0 reduce-scatter.3.cloned.1.call-start
  38.4 37.7 %all-gather.5.cloned.1.call-done = bf16[1024,1024]{1,0:T(8,128)(2,1)} async-done(((bf16[1024,128]{1,0:T(8,128)(2,1)}), bf16[1024,1024]{1,0:T(8,128)(2,1)}) %all-gather.5.cloned.1.call-update) | async-done | bytes 2097168 | tf_op jit(solution)/shard_map/all_gather | solution.py:32
  76.1 2.1 fusion
  78.2 36.4 %all-gather.7.cloned.1.call-done = bf16[2048,1024]{1,0:T(8,128)(2,1)} async-done(((bf16[128,1024]{1,0:T(8,128)(2,1)}), bf16[2048,1024]{1,0:T(8,128)(2,1)}) %all-gather.7.cloned.1.call-update) | async-done | bytes 4194320 | tf_op jit(solution)/shard_map/all_gather | solution.py:39
  114.6 7.2 %multiply_reduce_fusion = (f32[1024]{0:T(1024)S(1)}, f32[1024,2048]{1,0:T(8,128)S(1)}) fusion(bf16[2048,1024]{1,0:T(8,128)(2,1)} %all-gather.7.cloned.1.call-done, f32[1024]{0:T(1024)S(1)} %add_sqrt_fusion, bf16[1024,1024]{1,0:T(8,128)(2,1)} %all-gather.5.cloned.1.call-done), kind=kOutput, calls=%fused_computation.4 | convolution fusion | flops 4302306304 | bytes 14688256 | tf_op jit(solution)/shard_map/dot_general | solution.py:41
  121.8 4.2 %exponential_reduce_fusion = (f32[1024]{0:T(1024)S(1)}, f32[1024]{0:T(1024)S(1)}) fusion(f32[1024,2048]{1,0:T(8,128)S(1)} %get-tuple-element.14, f32[1024]{0:T(1024)S(1)} %get-tuple-element.13, s32[1024]{0:T(1024)S(1)} %bitcast.43), kind=kLoop, calls=%fused_computation.3 | loop fusion | flops 12580864 | bytes 8404992 | tf_op jit(solution)/shard_map/reduce_sum | solution.py:52
  126.0 34.3 %all-gather.1 = f32[8,3,1024]{2,1,0:T(4,128)S(1)} all-gather(f32[1,3,1024]{2,1,0:T(4,128)S(1)} %maximum_bitcast_fusion), channel_id=2, replica_groups=mesh['dp'=16,'tensor'=8] {'tensor'}, dimensions={0}, use_global_device_ids=true | all-gather | bytes 110592 | tf_op jit(solution)/shard_map/all_gather | solution.py:55
  160.4 0.1 fusion.11
  160.6 7.1 %convolution_multiply_fusion.1 = f32[1024,1024]{1,0:T(8,128)} fusion(bf16[2048,1024]{1,0:T(8,128)(2,1)S(1)} %copy-done.4, f32[1024,2048]{1,0:T(8,128)S(1)} %get-tuple-element.14, f32[1024]{0:T(1024)S(1)} %get-tuple-element.8, s32[1024]{0:T(1024)S(1)} %bitcast.44), kind=kOutput, calls=%fused_computation.9 | convolution fusion | flops 4308598784 | bytes 16785408 | tf_op jit(solution)/shard_map/dot_general | solution.py:67
  167.6 0.0 reduce-scatter.3.cloned.1.call-update
  167.7 0.2 reduce-scatter.5.cloned.1.call-start
  167.9 12.6 %convolution_multiply_fusion = f32[2048,1024]{1,0:T(8,128)} fusion(f32[1024,2048]{1,0:T(8,128)} %copy-done.1, f32[1024]{0:T(1024)S(1)} %get-tuple-element.8, s32[1024]{0:T(1024)S(1)} %bitcast.45, bf16[1024,1024]{1,0:T(8,128)(2,1)S(1)} %copy-done.2, f32[1024]{0:T(1024)S(1)} %add_sqrt_fusion), kind=kOutput, calls=%fused_computation.7 | convolution fusion | flops 4312793088 | bytes 18886656 | tf_op jit(solution)/shard_map/dot_general | solution.py:63
  180.6 0.0 reduce-scatter.5.cloned.1.call-update
  180.6 0.1 dynamic-slice.3
  180.7 2.6 convert_divide_fusion
  183.3 0.6 dynamic_slice.7
  183.9 68.8 %reduce-scatter.3.cloned.1.call-done = f32[128,1024]{1,0:T(8,128)} async-done(((f32[1024,1024]{1,0:T(8,128)}), f32[128,1024]{1,0:T(8,128)}) %reduce-scatter.3.cloned.1.call-update) | async-done | bytes 524304 | tf_op jit(solution)/shard_map/reduce_scatter | solution.py:68
  252.7 1.3 multiply_reduce_fusion.2
  254.0 2.1 subtract_divide_fusion.1
  256.1 72.8 %reduce-scatter.5.cloned.1.call-done = f32[128,1024]{1,0:T(8,128)} async-done(((f32[2048,1024]{1,0:T(8,128)}), f32[128,1024]{1,0:T(8,128)}) %reduce-scatter.5.cloned.1.call-update) | async-done | bytes 524304 | tf_op jit(solution)/shard_map/reduce_scatter | solution.py:66
  328.9 1.3 multiply_reduce_fusion.1
  330.2 2.0 subtract_divide_fusion
  (15 shorter events, 0.1 us)
Async XLA Ops:
  7.2 1.2 copy-start
  7.2 68.9 %all-gather.5.cloned.1.call-start = ((), (), s32[]{:S(2)}) async-start(), calls=%async_computation.3 | async-start | bytes 2359296 | tf_op jit(solution)/shard_map/all_gather | solution.py:32
  14.8 23.5 %copy-start.3 = (s32[1,1024]{1,0:T(1,128)S(1)}, s32[1,1024]{1,0:T(1,128)}, u32[]{:S(2)}) copy-start(s32[1,1024]{1,0:T(1,128)} %param.7) | copy-start | bytes 12292
  14.8 99.7 %all-gather.7.cloned.1.call-start = ((), (), s32[]{:S(2)}) async-start(), calls=%async_computation.4 | async-start | bytes 4456448 | tf_op jit(solution)/shard_map/all_gather | solution.py:39
  38.3 214.4 %reduce-scatter.3.cloned.1.call-start = ((), (), s32[]{:S(2)}) async-start(), calls=%async_computation.5 | async-start | bytes 4718592 | tf_op jit(solution)/shard_map/reduce_scatter | solution.py:68
  121.8 38.8 %copy-start.1 = (f32[1024,2048]{1,0:T(8,128)}, f32[1024,2048]{1,0:T(8,128)S(1)}, u32[]{:S(2)}) copy-start(f32[1024,2048]{1,0:T(8,128)S(1)} %get-tuple-element.14) | copy-start | bytes 25165828
  121.8 38.8 %copy-start.4 = (bf16[2048,1024]{1,0:T(8,128)(2,1)S(1)}, bf16[2048,1024]{1,0:T(8,128)(2,1)}, u32[]{:S(2)}) copy-start(bf16[2048,1024]{1,0:T(8,128)(2,1)} %all-gather.7.cloned.1.call-done) | copy-start | bytes 12582916
  160.6 7.3 %copy-start.2 = (bf16[1024,1024]{1,0:T(8,128)(2,1)S(1)}, bf16[1024,1024]{1,0:T(8,128)(2,1)}, u32[]{:S(2)}) copy-start(bf16[1024,1024]{1,0:T(8,128)(2,1)} %all-gather.5.cloned.1.call-done) | copy-start | bytes 6291460
  167.7 161.2 %reduce-scatter.5.cloned.1.call-start = ((), (), s32[]{:S(2)}) async-start(), calls=%async_computation.6 | async-start | bytes 8912896 | tf_op jit(solution)/shard_map/reduce_scatter | solution.py:66
Sparse Core Ops, SparseCore 0:
  15.0 61.0 all-gather.4
  78.4 36.1 all-gather.6
  167.8 84.8 reduce-scatter.2
  254.9 73.9 reduce-scatter.4
